TPU v7x, 256 devices: a whole 4x4x8 slice. The times are simulated.
256 devices in a mesh: row: 8 (over x, core), col: 32 (over z, y).
Axes of the slice: x: 4, y: 4, z: 8, core: 2. Of those that a mesh axis runs over, the one named last changes fastest.
Arguments:
- inputs: bfloat16 [1024, 8192], P('col', 'row'), may hold values from -6 to 6
- target: bfloat16 [1024, 8192], P(None, 'row'), may hold values from -6 to 6
- gate_weight: bfloat16 [8192, 16384], P('row', 'col'), may hold values from -0.0625 to 0.0625
- up_weight: bfloat16 [8192, 16384], P('row', 'col'), may hold values from -0.0625 to 0.0625
- down_weight: bfloat16 [16384, 8192], P('col', 'row'), may hold values from -0.046875 to 0.046875
Outputs:
- output: bfloat16 [1024, 8192], P('col', 'row')
- grad_inputs: bfloat16 [1024, 8192], P('col', 'row')
- grad_gate_weight: bfloat16 [8192, 16384], P('row', 'col')
- grad_up_weight: bfloat16 [8192, 16384], P('row', 'col')
- grad_down_weight: bfloat16 [16384, 8192], P('col', 'row')
All inputs are finite; a program needn't handle non-finite values.
Results may differ from a plain program's by a relative error of at most 0.0065.
Values may be sent and summed in bfloat16 or wider, within the bound.
No kernel may reach another device: no remote copies, remote signals or barrier semaphores. Data moves between devices by JAX's collectives and lax.ppermute only.
A program may use at most 64 MiB of HBM per device.

v0:
```python
import jax
import jax.numpy as jnp
from jax import lax
from jax.sharding import PartitionSpec as P


def contract_first(left, right):
    return lax.dot_general(
        left, right, (((0,), (0,)), ((), ())), preferred_element_type=jnp.float32
    )


def contract_last(left, right):
    return lax.dot_general(
        left, right, (((1,), (1,)), ((), ())), preferred_element_type=jnp.float32
    )


def gate_grads(hidden_grad, gate_act, up_act):
    sigma = jax.nn.sigmoid(gate_act)
    silu_val = gate_act * sigma
    grad_gate = (hidden_grad * up_act * sigma * (1.0 + gate_act * (1.0 - sigma))).astype(
        jnp.bfloat16
    )
    grad_up = (hidden_grad * silu_val).astype(jnp.bfloat16)
    return (grad_gate, grad_up)


def body(inputs, target, gate_weight, up_weight, down_weight):
    tokens_all = lax.all_gather(inputs, "col", axis=0, tiled=True)
    gate_part = jnp.dot(tokens_all, gate_weight, preferred_element_type=jnp.float32)
    up_part = jnp.dot(tokens_all, up_weight, preferred_element_type=jnp.float32)
    gate_own, up_own = (
        lax.psum_scatter(gate_part, "row", scatter_dimension=0, tiled=True),
        lax.psum_scatter(up_part, "row", scatter_dimension=0, tiled=True),
    )
    hidden_own = (jax.nn.silu(gate_own) * up_own).astype(jnp.bfloat16)
    hidden_all = lax.all_gather(hidden_own, "row", axis=0, tiled=True)
    result_part = jnp.dot(hidden_all, down_weight, preferred_element_type=jnp.float32)
    tok_col = inputs.shape[0]
    offset = lax.axis_index("col") * tok_col
    result_own = lax.psum_scatter(result_part, "col", scatter_dimension=0, tiled=True)
    target_own = lax.dynamic_slice_in_dim(target, offset, tok_col, 0)
    error_own = (result_own - target_own.astype(jnp.float32)).astype(jnp.bfloat16)
    output = result_own.astype(jnp.bfloat16)
    error_all = lax.all_gather(error_own, "col", axis=0, tiled=True)
    grad_down_weight = contract_first(hidden_all, error_all).astype(jnp.bfloat16)
    hidden_grad_part = contract_last(error_all, down_weight)
    hidden_grad = lax.psum_scatter(hidden_grad_part, "row", scatter_dimension=0, tiled=True)
    gate_grad_own, up_grad_own = gate_grads(hidden_grad, gate_own, up_own)
    gate_grad_all, up_grad_all = (
        lax.all_gather(gate_grad_own, "row", axis=0, tiled=True),
        lax.all_gather(up_grad_own, "row", axis=0, tiled=True),
    )
    grad_gate_weight = contract_first(tokens_all, gate_grad_all).astype(jnp.bfloat16)
    grad_up_weight = contract_first(tokens_all, up_grad_all).astype(jnp.bfloat16)
    input_grad_part = contract_last(gate_grad_all, gate_weight) + contract_last(
        up_grad_all, up_weight
    )
    grad_inputs = lax.psum_scatter(input_grad_part, "col", scatter_dimension=0, tiled=True).astype(
        jnp.bfloat16
    )
    return (output, grad_inputs, grad_gate_weight, grad_up_weight, grad_down_weight)


def solution(mesh):
    placed = (P("col", "row"), P(None, "row"), P("row", "col"), P("row", "col"), P("col", "row"))
    return jax.shard_map(
        body,
        mesh=mesh,
        in_specs=placed,
        out_specs=(
            P("col", "row"),
            P("col", "row"),
            P("row", "col"),
            P("row", "col"),
            P("col", "row"),
        ),
        check_vma=False,
    )
```

profile of v0, /device:TPU:4, one launch (start us, length us, event | category | flops | bytes accessed | tf_op | source)
XLA Modules:
  0.0 833.2 jit_solution(12145454576737987996)
XLA Ops:
  7.2 0.0 copy-start
  7.2 0.0 all-gather.6.cloned.1.call-start
  7.2 0.7 all-gather.6.cloned.1.call-update
  7.9 0.0 reduce-scatter.8.cloned.1.call-start
  8.0 83.7 %all-gather.6.cloned.1.call-done = bf16[1024,1024]{1,0:T(8,128)(2,1)} async-done(((bf16[32,1024]{1,0:T(8,128)(2,1)}), bf16[1024,1024]{1,0:T(8,128)(2,1)}) %all-gather.6.cloned.1.call-update) | async-done | bytes 2097168 | tf_op jit(solution)/shard_map/all_gather | solution.py:30
  91.7 4.4 fusion.4
  96.1 0.0 reduce-scatter.8.cloned.1.call-update
  96.1 0.0 reduce-scatter.6.cloned.1.call-start
  96.2 1.5 copy-done.1
  97.7 3.8 fusion.3
  101.5 0.0 reduce-scatter.6.cloned.1.call-update
  101.5 0.0 all-gather.8.cloned.1.call-start
  101.5 23.3 %reduce-scatter.8.cloned.1.call-done = f32[128,512]{1,0:T(8,128)} async-done(((f32[1024,512]{1,0:T(8,128)}), f32[128,512]{1,0:T(8,128)}) %reduce-scatter.8.cloned.1.call-update) | async-done | bytes 262160 | tf_op jit(solution)/shard_map/reduce_scatter | solution.py:35
  124.8 37.8 %reduce-scatter.6.cloned.1.call-done = f32[128,512]{1,0:T(8,128)} async-done(((f32[1024,512]{1,0:T(8,128)}), f32[128,512]{1,0:T(8,128)}) %reduce-scatter.6.cloned.1.call-update) | async-done | bytes 262160 | tf_op jit(solution)/shard_map/reduce_scatter | solution.py:34
  162.7 1.8 multiply_convert_fusion.2
  164.4 0.0 all-gather.8.cloned.1.call-update
  164.5 0.0 reduce-scatter.10.cloned.1.call-start
  164.5 28.6 %all-gather.8.cloned.1.call-done = bf16[1024,512]{1,0:T(8,128)(2,1)} async-done(((bf16[128,512]{1,0:T(8,128)(2,1)}), bf16[1024,512]{1,0:T(8,128)(2,1)}) %all-gather.8.cloned.1.call-update) | async-done | bytes 1048592 | tf_op jit(solution)/shard_map/all_gather | solution.py:38
  193.1 4.4 fusion.5
  197.5 0.0 reduce-scatter.10.cloned.1.call-update
  197.5 0.0 all-gather.10.cloned.1.call-start
  197.6 224.9 %reduce-scatter.10.cloned.1.call-done = f32[32,1024]{1,0:T(8,128)} async-done(((f32[1024,1024]{1,0:T(8,128)}), f32[32,1024]{1,0:T(8,128)}) %reduce-scatter.10.cloned.1.call-update) | async-done | bytes 131088 | tf_op jit(solution)/shard_map/reduce_scatter | solution.py:42
  422.5 1.7 subtract_convert_fusion
  424.1 0.0 all-gather.10.cloned.1.call-update
  424.2 0.0 reduce-scatter.12.cloned.1.call-start
  424.2 77.6 %all-gather.10.cloned.1.call-done = bf16[1024,1024]{1,0:T(8,128)(2,1)} async-done(((bf16[32,1024]{1,0:T(8,128)(2,1)}), bf16[1024,1024]{1,0:T(8,128)(2,1)}) %all-gather.10.cloned.1.call-update) | async-done | bytes 2097168 | tf_op jit(solution)/shard_map/all_gather | solution.py:46
  501.8 4.2 fusion.6
  506.0 0.0 reduce-scatter.12.cloned.1.call-update
  506.0 0.0 all-gather.12.cloned.1.call-start
  506.1 28.7 %reduce-scatter.12.cloned.1.call-done = f32[128,512]{1,0:T(8,128)} async-done(((f32[1024,512]{1,0:T(8,128)}), f32[128,512]{1,0:T(8,128)}) %reduce-scatter.12.cloned.1.call-update) | async-done | bytes 262160 | tf_op jit(solution)/shard_map/reduce_scatter | solution.py:49
  534.7 0.0 copy-done.3
  534.7 1.9 multiply_convert_fusion
  536.6 0.0 all-gather.12.cloned.1.call-update
  536.6 0.0 all-gather.14.cloned.1.call-start
  536.7 0.7 all-gather.14.cloned.1.call-update
  537.4 0.0 reduce-scatter.14.cloned.1.call-start
  537.4 27.9 %all-gather.12.cloned.1.call-done = bf16[1024,512]{1,0:T(8,128)(2,1)} async-done(((bf16[128,512]{1,0:T(8,128)(2,1)}), bf16[1024,512]{1,0:T(8,128)(2,1)}) %all-gather.12.cloned.1.call-update) | async-done | bytes 1048592 | tf_op jit(solution)/shard_map/all_gather | solution.py:52
  565.4 4.8 fusion.7
  570.1 23.4 %all-gather.14.cloned.1.call-done = bf16[1024,512]{1,0:T(8,128)(2,1)} async-done(((bf16[128,512]{1,0:T(8,128)(2,1)}), bf16[1024,512]{1,0:T(8,128)(2,1)}) %all-gather.14.cloned.1.call-update) | async-done | bytes 1048592 | tf_op jit(solution)/shard_map/all_gather | solution.py:53
  593.5 6.1 convolution_add_fusion
  599.6 0.0 reduce-scatter.14.cloned.1.call-update
  599.6 4.2 convolution_convert_fusion
  603.8 2.3 fusion.1
  606.1 2.3 copy.11
  608.4 3.5 fusion
  611.9 2.3 copy.10
  614.1 210.7 %reduce-scatter.14.cloned.1.call-done = f32[32,1024]{1,0:T(8,128)} async-done(((f32[1024,1024]{1,0:T(8,128)}), f32[32,1024]{1,0:T(8,128)}) %reduce-scatter.14.cloned.1.call-update) | async-done | bytes 131088 | tf_op jit(solution)/shard_map/reduce_scatter | solution.py:60
  824.8 1.5 convert_element_type.42
  (5 shorter events, 0.0 us)
Async XLA Ops:
  7.2 185.9 %copy-start = (bf16[512,1024]{1,0:T(8,128)(2,1)S(1)}, bf16[512,1024]{1,0:T(8,128)(2,1)}, u32[]{:S(2)}) copy-start(bf16[512,1024]{1,0:T(8,128)(2,1)} %param.9) | copy-start | bytes 3145732
  7.2 84.5 %all-gather.6.cloned.1.call-start = ((), (), s32[]{:S(2)}) async-start(), calls=%async_computation.5 | async-start | bytes 2162688 | tf_op jit(solution)/shard_map/all_gather | solution.py:30
  7.9 116.9 %reduce-scatter.8.cloned.1.call-start = ((), (), s32[]{:S(2)}) async-start(), calls=%async_computation.7 | async-start | bytes 2359296 | tf_op jit(solution)/shard_map/reduce_scatter | solution.py:35
  96.1 1.6 copy-start.1
  96.1 66.5 %reduce-scatter.6.cloned.1.call-start = ((), (), s32[]{:S(2)}) async-start(), calls=%async_computation.6 | async-start | bytes 2359296 | tf_op jit(solution)/shard_map/reduce_scatter | solution.py:34
  101.5 91.6 %all-gather.8.cloned.1.call-start = ((), (), s32[]{:S(2)}) async-start(), calls=%async_computation.8 | async-start | bytes 1179648 | tf_op jit(solution)/shard_map/all_gather | solution.py:38
  164.5 258.0 %reduce-scatter.10.cloned.1.call-start = ((), (), s32[]{:S(2)}) async-start(), calls=%async_computation.9 | async-start | bytes 4325376 | tf_op jit(solution)/shard_map/reduce_scatter | solution.py:42
  197.5 304.3 %all-gather.10.cloned.1.call-start = ((), (), s32[]{:S(2)}) async-start(), calls=%async_computation.10 | async-start | bytes 2162688 | tf_op jit(solution)/shard_map/all_gather | solution.py:46
  424.2 110.6 %reduce-scatter.12.cloned.1.call-start = ((), (), s32[]{:S(2)}) async-start(), calls=%async_computation.11 | async-start | bytes 2359296 | tf_op jit(solution)/shard_map/reduce_scatter | solution.py:49
  506.0 28.7 %copy-start.3 = (f32[128,512]{1,0:T(8,128)S(1)}, f32[128,512]{1,0:T(8,128)}, u32[]{:S(2)}) copy-start(f32[128,512]{1,0:T(8,128)} %reduce-scatter.8.cloned.1.call-done) | copy-start | bytes 786436
  506.0 59.3 %all-gather.12.cloned.1.call-start = ((), (), s32[]{:S(2)}) async-start(), calls=%async_computation.12 | async-start | bytes 1179648 | tf_op jit(solution)/shard_map/all_gather | solution.py:52
  536.6 56.9 %all-gather.14.cloned.1.call-start = ((), (), s32[]{:S(2)}) async-start(), calls=%async_computation.13 | async-start | bytes 1179648 | tf_op jit(solution)/shard_map/all_gather | solution.py:53
  537.4 287.5 %reduce-scatter.14.cloned.1.call-start = ((), (), s32[]{:S(2)}) async-start(), calls=%async_computation.14 | async-start | bytes 4325376 | tf_op jit(solution)/shard_map/reduce_scatter | solution.py:60
  599.6 4.2 copy-start.2
Sparse Core Ops, SparseCore 0:
  10.6 81.0 all-gather.5
  96.3 28.5 reduce-scatter.7
  127.4 35.2 reduce-scatter.5
  165.0 28.0 all-gather.7
  197.6 224.8 reduce-scatter.9
  425.5 76.2 all-gather.9
  506.1 28.5 reduce-scatter.11
  537.2 28.1 all-gather.11
  567.8 25.6 all-gather.13
  599.7 225.0 reduce-scatter.13
where the time goes:
time: 834 us; the launch traced here: 833 us
  waiting for transfers between devices  768 us (92%)
  matrix products  37.6 us (5%)
  between operations  14.2 us (2%)
    reduce_scatter x1, waiting for transfers between devices, body(): lax.psum_scatter(result_part, 'col', scatter_dimension=0, tiled=True)  225 us
    reduce_scatter x1, waiting for transfers between devices, body(): lax.psum_scatter(input_grad_part, 'col', scatter_dimension=0, tiled=True)  211 us
    all_gather x1, waiting for transfers between devices, body(): tokens_all = lax.all_gather(inputs, 'col', axis=0, tiled=True)  83.7 us
    all_gather x1, waiting for transfers between devices, body(): error_all = lax.all_gather(error_own, 'col', axis=0, tiled=True)  77.6 us
    reduce_scatter x1, waiting for transfers between devices, body(): lax.psum_scatter(gate_part, 'row', scatter_dimension=0, tiled=True)  37.8 us
    reduce_scatter x1, waiting for transfers between devices, body(): lax.psum_scatter(hidden_grad_part, 'row', scatter_dimension=0, tiled=True)  28.7 us
    all_gather x1, waiting for transfers between devices, body(): hidden_all = lax.all_gather(hidden_own, 'row', axis=0, tiled=True)  28.6 us
    all_gather x1, waiting for transfers between devices, body(): lax.all_gather(gate_grad_own, 'row', axis=0, tiled=True)  27.9 us
  transfers between devices with their start and end apart: 10, of which 10 were waited for; matrix products, arithmetic and copies ran while one was open for 3% of the time, Pallas kernels for 0%

commit v1 on v0

v1 whole, which is shorter than its diff:
```python
import jax
import jax.numpy as jnp
from jax import lax
from jax.sharding import Mesh, PartitionSpec as P

F32 = jnp.float32
BF16 = jnp.bfloat16
NX, NC, NZ, NY = 4, 2, 8, 4


def contract_first(left, right):
    return lax.dot_general(left, right, (((0,), (0,)), ((), ())), preferred_element_type=F32)


def contract_last(left, right):
    return lax.dot_general(left, right, (((1,), (1,)), ((), ())), preferred_element_type=F32)


def exchange(val, axis):
    return lax.all_to_all(val, axis, split_axis=0, concat_axis=0, tiled=True)


def scatter_sum(part, axis, size):
    rows, cols = part.shape
    got = exchange(part.astype(BF16), axis).reshape(size, rows // size, cols)
    return jnp.sum(got.astype(F32), axis=0)


def spread(own, axis, size):
    rows, cols = own.shape
    return exchange(jnp.broadcast_to(own[None], (size, rows, cols)).reshape(size * rows, cols), axis)


def gather_col(own):
    return lax.all_gather(spread(own, "z", NZ), "y", axis=0, tiled=True)


def scatter_col(part):
    return scatter_sum(scatter_sum(part, "y", NY), "z", NZ)


def swap_core(val):
    return lax.ppermute(val, "core", [(0, 1), (1, 0)])


def scatter_row(part):
    half = part.shape[0] // NC
    core = lax.axis_index("core")
    mine = lax.dynamic_slice_in_dim(part, core * half, half, 0)
    other = lax.dynamic_slice_in_dim(part, (1 - core) * half, half, 0)
    both = mine + swap_core(other.astype(BF16)).astype(F32)
    return scatter_sum(both, "x", NX)


def gather_row(own):
    mine = spread(own, "x", NX)
    other = swap_core(mine)
    first = lax.axis_index("core") == 0
    return jnp.concatenate([jnp.where(first, mine, other), jnp.where(first, other, mine)], axis=0)


def gate_grads(hidden_grad, gate_act, up_act):
    sigma = jax.nn.sigmoid(gate_act)
    silu_val = gate_act * sigma
    grad_gate = hidden_grad * up_act * sigma * (1.0 + gate_act * (1.0 - sigma))
    grad_up = hidden_grad * silu_val
    return jnp.concatenate([grad_gate.astype(BF16), grad_up.astype(BF16)], axis=1)


def body(inputs, target, gate_weight, up_weight, down_weight):
    wide = gate_weight.shape[1]
    tok_own = inputs.shape[0]
    tokens_all = gather_col(inputs)
    gate_part = jnp.dot(tokens_all, gate_weight, preferred_element_type=F32)
    up_part = jnp.dot(tokens_all, up_weight, preferred_element_type=F32)
    acts = scatter_row(jnp.concatenate([gate_part, up_part], axis=1))
    gate_own, up_own = acts[:, :wide], acts[:, wide:]
    hidden_own = (jax.nn.silu(gate_own) * up_own).astype(BF16)
    hidden_all = gather_row(hidden_own)
    result_part = jnp.dot(hidden_all, down_weight, preferred_element_type=F32)
    result_own = scatter_col(result_part)
    offset = (lax.axis_index("z") * NY + lax.axis_index("y")) * tok_own
    target_own = lax.dynamic_slice_in_dim(target, offset, tok_own, 0)
    error_own = (result_own - target_own.astype(F32)).astype(BF16)
    output = result_own.astype(BF16)
    error_all = gather_col(error_own)
    hidden_grad = scatter_row(contract_last(error_all, down_weight))
    grads_all = gather_row(gate_grads(hidden_grad, gate_own, up_own))
    gate_grad_all, up_grad_all = grads_all[:, :wide], grads_all[:, wide:]
    input_grad_part = contract_last(gate_grad_all, gate_weight) + contract_last(
        up_grad_all, up_weight
    )
    grad_inputs = scatter_col(input_grad_part).astype(BF16)
    grad_down_weight = contract_first(hidden_all, error_all).astype(BF16)
    grad_gate_weight = contract_first(tokens_all, gate_grad_all).astype(BF16)
    grad_up_weight = contract_first(tokens_all, up_grad_all).astype(BF16)
    return (output, grad_inputs, grad_gate_weight, grad_up_weight, grad_down_weight)


def solution(mesh):
    fine = Mesh(mesh.devices.reshape(NX, NC, NZ, NY), ("x", "core", "z", "y"))
    row, col = ("x", "core"), ("z", "y")
    placed = (P(col, row), P(None, row), P(row, col), P(row, col), P(col, row))
    return jax.shard_map(
        body,
        mesh=fine,
        in_specs=placed,
        out_specs=(P(col, row), P(col, row), P(row, col), P(row, col), P(col, row)),
        check_vma=False,
    )
```

time: 834 us -> 319 us (0.38)
  waiting for transfers between devices: 768 us -> 85.8 us
  blocking collectives: 0 us -> 161 us
  matrix products: 37.6 us -> 21.7 us
  starting transfers between devices: 0.41 us -> 14.2 us
    reduce_scatter x5 -> x0, waiting for transfers between devices: 525 us -> none  [the longest x1 225 us: body(): lax.psum_scatter(result_part, 'col', scatter_dimension=0, tiled=True)]
    all_gather x5 -> x2, waiting for transfers between devices: 241 us -> 57.9 us  [gather_col(): return lax.all_gather(spread(own, 'z', NZ), 'y', axis=0, tiled=True)]
    all_to_all x0 -> x8, blocking collectives: none -> 161 us  [exchange(): return lax.all_to_all(val, axis, split_axis=0, concat_axis=0, tiled=True)]
    all_to_all x0 -> x2, waiting for transfers between devices: none -> 18.4 us  [exchange(): return lax.all_to_all(val, axis, split_axis=0, concat_axis=0, tiled=True)]
    all_to_all x0 -> x2, starting transfers between devices: none -> 14 us  [exchange(): return lax.all_to_all(val, axis, split_axis=0, concat_axis=0, tiled=True)]
    dot_general x3, matrix products: 15 us -> 5.44 us  [contract_last(): lax.dot_general(left, right, (((1,), (1,)), ((), ())), preferred_element_...]
    ppermute x0 -> x4, waiting for transfers between devices: none -> 9.46 us  [swap_core(): return lax.ppermute(val, 'core', [(0, 1), (1, 0)])]
  transfers between devices with their start and end apart: 10 -> 8, of which waited for: 10 -> 8; matrix products, arithmetic and copies ran while one was open for 3% -> 5% of each run, Pallas kernels for 0% -> 0%
where the time goes in v1:
time: 319 us; the launch traced here: 316 us
  blocking collectives  161 us (50%)
  waiting for transfers between devices  85.8 us (27%)
  matrix products  21.7 us (7%)
  between operations  14.3 us (4%)
  starting transfers between devices  14.2 us (4%)
  other arithmetic  11.6 us (4%)
  local copies, waits for them, and re-layouts  7.41 us (2%)
    all_to_all x8, blocking collectives, exchange(): return lax.all_to_all(val, axis, split_axis=0, concat_axis=0, tiled=True)  161 us
    all_gather x2, waiting for transfers between devices, gather_col(): return lax.all_gather(spread(own, 'z', NZ), 'y', axis=0, tiled=True)  57.9 us
    all_to_all x2, waiting for transfers between devices, exchange(): return lax.all_to_all(val, axis, split_axis=0, concat_axis=0, tiled=True)  18.4 us
    all_to_all x2, starting transfers between devices, exchange(): return lax.all_to_all(val, axis, split_axis=0, concat_axis=0, tiled=True)  14 us
    dot_general x3, matrix products, contract_first(): lax.dot_general(left, right, (((0,), (0,)), ((), ())), preferred_element_...  10.4 us
    ppermute x4, waiting for transfers between devices, swap_core(): return lax.ppermute(val, 'core', [(0, 1), (1, 0)])  9.46 us
  transfers between devices with their start and end apart: 8, of which 8 were waited for; matrix products, arithmetic and copies ran while one was open for 5% of the time, Pallas kernels for 0%

profile of v1, /device:TPU:4, one launch (start us, length us, event | category | flops | bytes accessed | tf_op | source)
XLA Modules:
  0.0 316.0 jit_solution(8181957383931177860)
XLA Ops:
  7.2 1.0 broadcast_in_dim.8
  8.2 25.9 %all_to_all.90 = bf16[8,32,1024]{2,1,0:T(8,128)(2,1)} all-to-all(bf16[8,32,1024]{2,1,0:T(8,128)(2,1)S(1)} %broadcast_in_dim.8), channel_id=1, replica_groups=mesh['x'=4,'core'=2,'z'=8,'y'=4] {'z'}, dimensions={0} | all-to-all | bytes 1048576 | tf_op jit(solution)/shard_map/all_to_all | solution.py:20
  34.1 29.8 %all-gather.3.cloned.1.call-done = bf16[1024,1024]{1,0:T(8,128)(2,1)} async-done(((bf16[256,1024]{1,0:T(8,128)(2,1)}), bf16[1024,1024]{1,0:T(8,128)(2,1)}) %all-gather.3.cloned.1.call-update) | async-done | bytes 2097168 | tf_op jit(solution)/shard_map/all_gather | solution.py:35
  63.9 3.3 %fusion.18 = f32[1024,512]{0,1:T(8,128)S(1)} fusion(bf16[1024,1024]{1,0:T(8,128)(2,1)} %all-gather.3.cloned.1.call-done, bf16[1024,512]{1,0:T(8,128)(2,1)} %param.8), kind=kOutput, calls=%fused_computation.45 | convolution fusion | flops 1073741824 | bytes 5242880 | tf_op jit(solution)/shard_map/dot_general | solution.py:75
  67.2 1.3 fusion.17
  68.5 1.3 fusion.1
  69.8 0.4 copy-done.1
  70.2 3.0 collective-permute-done
  73.2 1.7 copy_bitcast_fusion
  75.0 17.3 %all_to_all.91 = bf16[4,128,1024]{1,2,0:T(8,128)(2,1)S(1)} all-to-all(bf16[4,128,1024]{1,2,0:T(8,128)(2,1)S(1)} %copy_bitcast_fusion), channel_id=1, replica_groups=mesh['x'=4,'core'=2,'z'=8,'y'=4] {'x'}, dimensions={0} | all-to-all | bytes 2097152 | tf_op jit(solution)/shard_map/all_to_all | solution.py:20
  92.3 0.1 convert_reduce_fusion
  92.4 0.8 copy-done.2
  93.3 0.1 copy.28
  93.5 11.0 %all_to_all.92 = bf16[4,128,512]{2,1,0:T(8,128)(2,1)S(1)} all-to-all(bf16[4,128,512]{2,1,0:T(8,128)(2,1)S(1)} %broadcast_in_dim.9), channel_id=1, replica_groups=mesh['x'=4,'core'=2,'z'=8,'y'=4] {'x'}, dimensions={0} | all-to-all | bytes 1048576 | tf_op jit(solution)/shard_map/all_to_all | solution.py:20
  104.5 1.9 collective-permute-done.1
  106.4 0.1 broadcast_select_fusion.3
  106.6 1.3 convolution_convert_fusion
  107.8 29.5 %all_to_all.93 = bf16[4,256,1024]{2,1,0:T(8,128)(2,1)S(1)} all-to-all(bf16[4,256,1024]{2,1,0:T(8,128)(2,1)S(1)} %bitcast.38), channel_id=1, replica_groups=mesh['x'=4,'core'=2,'z'=8,'y'=4] {'y'}, dimensions={0} | all-to-all | bytes 4194304 | tf_op jit(solution)/shard_map/all_to_all | solution.py:20
  137.3 1.3 reduce_sum.64
  138.6 7.0 %all-to-all-start.4 = ((bf16[8,32,1024]{2,1,0:T(8,128)(2,1)}), bf16[8,32,1024]{2,1,0:T(8,128)(2,1)S(1)}, u32[]{:S(2)}, u32[]{:S(2)}) async-start(bf16[8,32,1024]{2,1,0:T(8,128)(2,1)} %bitcast.41), calls=%async_computation.4 | async-start | bytes 1048576 | tf_op jit(solution)/shard_map/all_to_all | solution.py:20
  145.7 16.3 %all-to-all-done.4 = bf16[8,32,1024]{2,1,0:T(8,128)(2,1)S(1)} async-done(((bf16[8,32,1024]{2,1,0:T(8,128)(2,1)}), bf16[8,32,1024]{2,1,0:T(8,128)(2,1)S(1)}, u32[]{:S(2)}, u32[]{:S(2)}) %all-to-all-start.4) | async-done | bytes 524320 | tf_op jit(solution)/shard_map/all_to_all | solution.py:20
  162.1 1.5 subtract_convert_fusion
  163.6 18.8 %all_to_all.94 = bf16[8,32,1024]{2,1,0:T(8,128)(2,1)} all-to-all(bf16[8,32,1024]{2,1,0:T(8,128)(2,1)S(1)} %broadcast_in_dim.10), channel_id=1, replica_groups=mesh['x'=4,'core'=2,'z'=8,'y'=4] {'z'}, dimensions={0} | all-to-all | bytes 1048576 | tf_op jit(solution)/shard_map/all_to_all | solution.py:20
  182.4 28.1 %all-gather.5.cloned.1.call-done = bf16[1024,1024]{1,0:T(8,128)(2,1)} async-done(((bf16[256,1024]{1,0:T(8,128)(2,1)}), bf16[1024,1024]{1,0:T(8,128)(2,1)}) %all-gather.5.cloned.1.call-update) | async-done | bytes 2097168 | tf_op jit(solution)/shard_map/all_gather | solution.py:35
  210.6 2.9 fusion.19
  213.5 0.1 collective-permute-start.2
  213.6 1.9 collective-permute-done.2
  215.5 0.2 add_convert_fusion.1
  215.7 11.7 %all_to_all.95 = bf16[4,128,512]{2,1,0:T(8,128)(2,1)S(1)} all-to-all(bf16[4,128,512]{2,1,0:T(8,128)(2,1)S(1)} %bitcast.37), channel_id=1, replica_groups=mesh['x'=4,'core'=2,'z'=8,'y'=4] {'x'}, dimensions={0} | all-to-all | bytes 1048576 | tf_op jit(solution)/shard_map/all_to_all | solution.py:20
  227.5 0.1 copy.29
  227.6 0.2 multiply_convert_fusion.1
  227.8 0.1 copy.31
  228.0 0.1 broadcast_in_dim.11
  228.1 16.7 %all_to_all.96 = bf16[4,128,1024]{2,1,0:T(8,128)(2,1)S(1)} all-to-all(bf16[4,128,1024]{2,1,0:T(8,128)(2,1)S(1)} %broadcast_in_dim.11), channel_id=1, replica_groups=mesh['x'=4,'core'=2,'z'=8,'y'=4] {'x'}, dimensions={0} | all-to-all | bytes 2097152 | tf_op jit(solution)/shard_map/all_to_all | solution.py:20
  244.8 2.7 collective-permute-done.3
  247.4 0.2 broadcast_select_fusion.1
  247.7 1.3 fusion.10
  248.9 1.3 add_convert_fusion
  250.2 30.1 %all_to_all.97 = bf16[4,256,1024]{2,1,0:T(8,128)(2,1)} all-to-all(bf16[4,256,1024]{2,1,0:T(8,128)(2,1)S(1)} %bitcast.34), channel_id=1, replica_groups=mesh['x'=4,'core'=2,'z'=8,'y'=4] {'y'}, dimensions={0} | all-to-all | bytes 4194304 | tf_op jit(solution)/shard_map/all_to_all | solution.py:20
  280.4 2.9 reduce_sum.67
  283.3 7.0 %all-to-all-start.9 = ((bf16[8,32,1024]{2,1,0:T(8,128)(2,1)}), bf16[8,32,1024]{2,1,0:T(8,128)(2,1)}, u32[]{:S(2)}, u32[]{:S(2)}) async-start(bf16[8,32,1024]{2,1,0:T(8,128)(2,1)} %bitcast.42), calls=%async_computation.9 | async-start | bytes 1048576 | tf_op jit(solution)/shard_map/all_to_all | solution.py:20
  290.4 4.3 %convolution_convert_fusion.1 = bf16[512,1024]{1,0:T(8,128)(2,1)} fusion(bf16[1024,1024]{1,0:T(8,128)(2,1)} %all-gather.5.cloned.1.call-done, bf16[512,512]{1,0:T(8,128)(2,1)} %copy-done.10, bf16[512,512]{1,0:T(8,128)(2,1)} %copy-done.9), kind=kOutput, calls=%fused_computation.14 | convolution fusion | flops 1076363264 | bytes 4194304 | tf_op jit(solution)/shard_map/dot_general | solution.py:12
  294.7 2.2 fusion.6
  296.9 2.3 copy.33
  299.2 3.9 %fusion.5 = bf16[1024,512]{0,1:T(8,128)(2,1)} fusion(bf16[1024,1024]{1,0:T(8,128)(2,1)} %all-gather.3.cloned.1.call-done, bf16[512,1024]{1,0:T(8,128)(2,1)S(1)} %get-tuple-element.25, bf16[512,1024]{1,0:T(8,128)(2,1)S(1)} %get-tuple-element.26), kind=kOutput, calls=%fused_computation.17 | convolution fusion | flops 1076363264 | bytes 5242880 | tf_op jit(solution)/shard_map/dot_general | solution.py:12
  303.0 2.3 copy.32
  305.3 2.1 all-to-all-done.9
  307.4 1.8 reduce_sum.68
  (34 shorter events, 0.6 us)
Async XLA Ops:
  7.2 99.4 %copy-start = (bf16[512,1024]{1,0:T(8,128)(2,1)S(1)}, bf16[512,1024]{1,0:T(8,128)(2,1)}, u32[]{:S(2)}) copy-start(bf16[512,1024]{1,0:T(8,128)(2,1)} %param.9) | copy-start | bytes 3145732
  7.2 56.7 %all-gather.3.cloned.1.call-start = ((), (), s32[]{:S(2)}) async-start(), calls=%async_computation.10 | async-start | bytes 2621440 | tf_op jit(solution)/shard_map/all_gather | solution.py:35
  63.9 3.3 %copy-start.4 = (bf16[1024,1024]{1,0:T(8,128)(2,1)S(1)}, bf16[1024,1024]{1,0:T(8,128)(2,1)}, u32[]{:S(2)}) copy-start(bf16[1024,1024]{1,0:T(8,128)(2,1)} %all-gather.3.cloned.1.call-done) | copy-start | bytes 6291460
  63.9 3.3 %copy-start.7 = (bf16[1024,512]{1,0:T(8,128)(2,1)S(1)}, bf16[1024,512]{1,0:T(8,128)(2,1)}, u32[]{:S(2)}) copy-start(bf16[1024,512]{1,0:T(8,128)(2,1)} %param.7) | copy-start | bytes 3145732
  68.5 1.7 copy-start.1
  70.2 3.0 collective-permute-start
  92.4 0.8 copy-start.2
  104.5 1.9 collective-permute-start.1
  106.5 1.3 copy-start.9
  106.5 1.3 copy-start.10
  138.6 23.4 %all-to-all-start.4 = ((bf16[8,32,1024]{2,1,0:T(8,128)(2,1)}), bf16[8,32,1024]{2,1,0:T(8,128)(2,1)S(1)}, u32[]{:S(2)}, u32[]{:S(2)}) async-start(bf16[8,32,1024]{2,1,0:T(8,128)(2,1)} %bitcast.41), calls=%async_computation.4 | async-start | bytes 1048576 | tf_op jit(solution)/shard_map/all_to_all | solution.py:20
  145.6 65.0 %all-gather.5.cloned.1.call-start = ((), (), s32[]{:S(2)}) async-start(), calls=%async_computation.11 | async-start | bytes 2621440 | tf_op jit(solution)/shard_map/all_gather | solution.py:35
  213.5 14.1 %copy-start.3 = (f32[128,1024]{0,1:T(8,128)S(1)}, f32[128,1024]{0,1:T(8,128)}, u32[]{:S(2)}) copy-start(f32[128,1024]{0,1:T(8,128)} %copy-done.2) | copy-start | bytes 1572868
  213.5 2.0 collective-permute-start.2
  244.8 2.9 copy-start.6
  244.8 2.7 collective-permute-start.3
  247.6 1.3 copy-start.8
  283.3 24.1 %all-to-all-start.9 = ((bf16[8,32,1024]{2,1,0:T(8,128)(2,1)}), bf16[8,32,1024]{2,1,0:T(8,128)(2,1)}, u32[]{:S(2)}, u32[]{:S(2)}) async-start(bf16[8,32,1024]{2,1,0:T(8,128)(2,1)} %bitcast.42), calls=%async_computation.9 | async-start | bytes 1048576 | tf_op jit(solution)/shard_map/all_to_all | solution.py:20
  290.4 4.3 %copy-start.5 = (bf16[1024,1024]{1,0:T(8,128)(2,1)S(1)}, bf16[1024,1024]{1,0:T(8,128)(2,1)}, u32[]{:S(2)}) copy-start(bf16[1024,1024]{1,0:T(8,128)(2,1)} %all-gather.3.cloned.1.call-done) | copy-start | bytes 6291460
Sparse Core Ops, SparseCore 0:
  34.2 29.6 all-gather.2
  182.6 27.9 all-gather.4
